TPU v7x, 128 devices: a whole 4x4x4 slice. The times are simulated.
128 devices in a mesh: seq: 32 (over z_hi, y, x), head: 4 (over z_lo, core).
Axes of the slice: x: 4, y: 4, z: 4 (z_hi: 2, z_lo: 2; z = z_hi * 2 + z_lo), core: 2. Of those that a mesh axis runs over, the one named last changes fastest.
Arguments:
- x_in: bfloat16 [16384, 4096], P('seq', 'head'), may hold values from -6 to 6
- z_in: bfloat16 [16384, 4096], P('seq', 'head'), may hold values from -6 to 6
- b_in: bfloat16 [16384, 512], P('seq', 'head'), may hold values from -0.5 to 0.5
- c_in: bfloat16 [16384, 512], P('seq', 'head'), may hold values from -0.5 to 0.5
- dt_raw: float32 [64, 16384], P('head', 'seq')
- dt_bias: float32 [64], P('head'), may hold values from -5 to -4
- a_log: float32 [64], P('head')
- d_skip: float32 [64], P('head'), may hold values from 0.1 to 1.9
- gain: float32 [4096], P('head'), may hold values from 0.5 to 1.5
- resets: int32 [64, 128], P('head', 'seq'), may hold values 0 or 1
- out_weight: bfloat16 [4096, 4096], P('seq', 'head'), may hold values from -0.09375 to 0.09375
- cotangent: bfloat16 [16384, 4096], P('seq', 'head'), may hold values from -6 to 6
Outputs:
- d_x: bfloat16 [16384, 4096], P('seq', 'head')
- d_z: bfloat16 [16384, 4096], P('seq', 'head')
- d_b: bfloat16 [16384, 512], P('seq', 'head')
- d_c: bfloat16 [16384, 512], P('seq', 'head')
- raw_timestep_gradient: float32 [64, 16384], P('head', 'seq')
- d_out_weight: float32 [4096, 4096], P('seq', 'head')
All inputs are finite; a program needn't handle non-finite values. No bound on the sum of `resets` on one device may be relied on, other than what follows from the above.
Results may differ from a plain program's by a relative error of at most 0.0075.
Values may be sent and summed in bfloat16 or wider, within the bound.
A program may use at most 256 MiB of HBM per device.

v0:
```python
from functools import partial
import jax
import jax.numpy as jnp
from jax import lax
from jax.sharding import PartitionSpec as P

HEADDIM = 64
STATE = 128
BLOCK = 128
highest = lax.Precision.HIGHEST


def prefix(value, axis, join, neutral, backward):
    count, mine = (lax.axis_size(axis), lax.axis_index(axis))
    pieces = jax.tree.map(lambda part: lax.all_gather(part, axis), value)
    if backward:
        pieces = jax.tree.map(lambda part: part[::-1], pieces)
        mine = count - 1 - mine
    so_far = jax.tree.map(
        lambda part, zero: jnp.full_like(part, 0) + jnp.asarray(zero, part.dtype), value, neutral
    )

    def step(position, so_far):
        longer = join(so_far, jax.tree.map(lambda part: part[position], pieces))
        return jax.tree.map(lambda new, old: jnp.where(position < mine, new, old), longer, so_far)

    return lax.fori_loop(0, count - 1, step, so_far)


def block_step(state, inputs, per_group, skip_gain):
    x_block, b_block, c_block, rate_block, step_block, keep_block = inputs
    running = jnp.cumsum(rate_block, axis=1)
    positions = rate_block.shape[1]
    lower = jnp.arange(positions)[:, None] >= jnp.arange(positions)[None, :]
    spread = jnp.where(lower[None], running[:, :, None] - running[:, None, :], 0.0)
    decays = jnp.exp(spread) * lower[None].astype(jnp.float32)
    scores = jnp.einsum("tgn,sgn->gts", c_block, b_block, precision=highest)
    scores = jnp.repeat(scores, per_group, axis=0)
    mixing = scores * decays * step_block[:, None, :]
    within = jnp.einsum("hts,shp->thp", mixing, x_block, precision=highest)
    c_heads = jnp.repeat(c_block, per_group, axis=1)
    b_heads = jnp.repeat(b_block, per_group, axis=1)
    carried = state * keep_block[:, None, None]
    incoming = (
        jnp.einsum("thn,hpn->thp", c_heads, carried, precision=highest)
        * jnp.exp(running).T[:, :, None]
    )
    output = within + incoming + skip_gain[None, :, None] * x_block
    weighted = (jnp.exp(running[:, -1:] - running) * step_block).T
    fresh = jnp.einsum("sh,shp,shn->hpn", weighted, x_block, b_heads, precision=highest)
    return (carried * jnp.exp(running[:, -1])[:, None, None] + fresh, output)


def scan_blocks(inputs, bmatrix, cmatrix, dt_raw, start, dt_bias, a_log, d_skip, keep):
    positions = inputs.shape[0]
    heads = dt_raw.shape[0]
    groups = bmatrix.shape[1] // STATE
    blocks = positions // BLOCK
    step_size = jax.nn.softplus(dt_raw + dt_bias[:, None])
    rate = -step_size * jnp.exp(a_log)[:, None]
    x_blocks = inputs.reshape(blocks, BLOCK, heads, HEADDIM)
    b_blocks = bmatrix.reshape(blocks, BLOCK, groups, STATE)
    c_blocks = cmatrix.reshape(blocks, BLOCK, groups, STATE)
    rate_blocks = rate.reshape(heads, blocks, BLOCK).transpose(1, 0, 2)
    step_blocks = step_size.reshape(heads, blocks, BLOCK).transpose(1, 0, 2)
    stepper = partial(block_step, per_group=heads // groups, skip_gain=d_skip)
    final, outputs = lax.scan(
        stepper, start, (x_blocks, b_blocks, c_blocks, rate_blocks, step_blocks, keep.T)
    )
    return (outputs.reshape(positions, heads * HEADDIM), final)


def gate_norm(mixed, gates, gain, groups):
    gated = mixed * jax.nn.silu(gates)
    count = gated.shape[0]
    grouped = gated.reshape(count, groups, -1)
    factor = lax.rsqrt(jnp.mean(grouped * grouped, axis=2, keepdims=True) + 1e-05)
    return (grouped * factor).reshape(count, -1) * gain


def compose(earlier, later):
    return (earlier[0] * later[0], later[0][:, None, None] * earlier[1] + later[1])


def body(
    x_in, z_in, b_in, c_in, dt_raw, dt_bias, a_log, d_skip, gain, resets, out_weight, cotangent
):
    heads = dt_raw.shape[0]
    groups = b_in.shape[1] // STATE
    per_group = heads // groups
    positions = x_in.shape[0]
    keep = 1.0 - resets.astype(jnp.float32)
    x_wide = x_in.astype(jnp.float32)
    input_matrix_wide = b_in.astype(jnp.float32)
    c_wide = c_in.astype(jnp.float32)
    z_wide = z_in.astype(jnp.float32)
    zero_state = jnp.zeros((heads, HEADDIM, STATE), jnp.float32)
    step_size = jax.nn.softplus(dt_raw + dt_bias[:, None])
    rate = -step_size * jnp.exp(a_log)[:, None]
    running = jnp.cumsum(rate, axis=1)
    suffix_rates = jnp.flip(jnp.cumsum(jnp.flip(rate, axis=1), axis=1), axis=1)
    after_rates = jnp.concatenate([suffix_rates[:, 1:], jnp.zeros((heads, 1), jnp.float32)], axis=1)
    keep_upto = jnp.repeat(jnp.cumprod(keep, axis=1), BLOCK, axis=1)
    keep_suffix = jnp.flip(jnp.cumprod(jnp.flip(keep, axis=1), axis=1), axis=1)
    keep_after = jnp.concatenate([keep_suffix[:, 1:], jnp.ones((heads, 1), jnp.float32)], axis=1)
    keep_after = jnp.repeat(keep_after, BLOCK, axis=1)
    to_end = jnp.exp(after_rates) * keep_after * step_size
    x_heads = x_wide.reshape(positions, groups, per_group, HEADDIM)
    b_groups = input_matrix_wide.reshape(positions, groups, STATE)
    c_groups = c_wide.reshape(positions, groups, STATE)
    end_weights = to_end.T.reshape(positions, groups, per_group)
    local_final = jnp.einsum(
        "tgq,tgqp,tgn->gqpn", end_weights, x_heads, b_groups, precision=highest
    ).reshape(heads, HEADDIM, STATE)
    slab_decay = jnp.exp(running[:, -1]) * jnp.prod(keep, axis=1)
    identity = (jnp.ones((heads,), jnp.float32), zero_state)
    entering = prefix((slab_decay, local_final), "seq", compose, identity, False)[1]

    def mixer(x_value, b_value, c_value, raw_steps, start_state):
        return scan_blocks(
            x_value, b_value, c_value, raw_steps, start_state, dt_bias, a_log, d_skip, keep
        )

    (mixed, leaving), mixer_pull = jax.vjp(
        mixer, x_wide, input_matrix_wide, c_wide, dt_raw, entering
    )

    def norming(mixed_value, z_value):
        return gate_norm(mixed_value, z_value, gain, groups)

    normed, norm_pull = jax.vjp(norming, mixed, z_wide)
    normed_half = normed.astype(jnp.bfloat16)
    gathered = lax.all_gather(cotangent, "head", axis=1, tiled=True)
    columns = gathered
    d_normed = jnp.dot(
        columns,
        lax.all_gather(out_weight, "seq", axis=0, tiled=True),
        preferred_element_type=jnp.float32,
    )
    d_mixed, grad_z = norm_pull(d_normed)
    from_start = (jnp.exp(running) * keep_upto).T.reshape(positions, groups, per_group)
    d_heads = d_mixed.reshape(positions, groups, per_group, HEADDIM)
    start_grad = jnp.einsum(
        "tgq,tgqp,tgn->gqpn", from_start, d_heads, c_groups, precision=highest
    ).reshape(heads, HEADDIM, STATE)
    arriving = prefix((slab_decay, start_grad), "seq", compose, identity, True)[1]
    grad_x, grad_b, grad_c, grad_steps, unused = mixer_pull((d_mixed, arriving))
    columns = gathered
    d_out_weight = lax.psum_scatter(
        jnp.einsum("td,ti->di", columns, normed_half, preferred_element_type=jnp.float32),
        "seq",
        scatter_dimension=0,
        tiled=True,
    )
    return (
        grad_x.astype(jnp.bfloat16),
        grad_z.astype(jnp.bfloat16),
        grad_b.astype(jnp.bfloat16),
        grad_c.astype(jnp.bfloat16),
        grad_steps,
        d_out_weight,
    )


def solution(mesh):
    return jax.shard_map(
        body,
        mesh=mesh,
        in_specs=(
            P("seq", "head"),
            P("seq", "head"),
            P("seq", "head"),
            P("seq", "head"),
            P("head", "seq"),
            P("head"),
            P("head"),
            P("head"),
            P("head"),
            P("head", "seq"),
            P("seq", "head"),
            P("seq", "head"),
        ),
        out_specs=(
            P("seq", "head"),
            P("seq", "head"),
            P("seq", "head"),
            P("seq", "head"),
            P("head", "seq"),
            P("seq", "head"),
        ),
        check_vma=False,
    )
```

profile of v0, /device:TPU:0, one launch (start us, length us, event | category | flops | bytes accessed | tf_op | source)
XLA Modules:
  0.0 738.4 jit_solution(9167421800133413308)
XLA Ops:
  21.2 96.0 %all-gather.2 = f32[32,1,16]{2,1,0:T(1,128)S(1)} all-gather(f32[1,1,16]{2,1,0:T(1,128)S(1)} %fusion.127), channel_id=1, replica_groups=mesh['seq'=32,'head'=4] {'seq'}, dimensions={0}, use_global_device_ids=true | all-gather | bytes 2112 | tf_op jit(solution)/shard_map/all_gather | solution.py:15
  120.9 54.4 %all-gather.12.cloned.1.call-done = f32[512,64,128]{2,1,0:T(8,128)} async-done(((f32[16,64,128]{2,1,0:T(8,128)}), f32[512,64,128]{2,1,0:T(8,128)}) %all-gather.12.cloned.1.call-update) | async-done | bytes 16777232 | tf_op jit(solution)/shard_map/all_gather | solution.py:15
  175.3 37.9 %while.110 = (s32[]{:T(128)}, f32[16,64,128]{2,1,0:T(8,128)S(1)}, s32[]{:T(128)}, f32[32,16]{1,0:T(8,128)S(1)}, f32[32,16,64,128]{3,2,1,0:T(8,128)}) while((s32[]{:T(128)}, f32[16,64,128]{2,1,0:T(8,128)S(1)}, s32[]{:T(128)}, f32[32,16]{1,0:T(8,128)S(1)}, f32[32,16,64,128]{3,2,1,0:T(8,128)}) %tuple.254), condition=%wide.region_8.9_spmd.clone.clone, body=%wide.region_7.8_spmd.clone.sunk.clone | while | flops 524292 | bytes 1573145 | solution.py:27
  216.0 83.1 %while.109 = (s32[]{:T(128)}, f32[16,64,128]{2,1,0:T(8,128)S(1)}, f32[4,128,16,64]{1,3,2,0:T(8,128)}, f32[4,16,128,128]{3,2,1,0:T(8,128)}, f32[4,16,128,128]{3,2...) while((s32[]{:T(128)}, f32[16,64,128]{2,1,0:T(8,128)S(1)}, ...), condition=%wide.region_11.12_spmd.clone.clone.clone, body=%wide.region_9.11_spmd.clone.clone.sunk.clone | while | flops 633511936 | bytes 16000793 | solution.py:67
  225.1 3.7 fusion.254
  245.9 3.7 fusion.254
  266.6 3.7 fusion.254
  281.3 3.2 multiply_dynamic-update-slice_fusion.3
  287.5 3.7 fusion.254
  299.2 4.7 copy.179
  303.9 4.8 reshape.531
  308.8 21.7 %all-gather.10.cloned.1.call-done = bf16[4096,1024]{1,0:T(8,128)(2,1)} async-done(((bf16[128,1024]{1,0:T(8,128)(2,1)}), bf16[4096,1024]{1,0:T(8,128)(2,1)}) %all-gather.10.cloned.1.call-update) | async-done | bytes 8388624 | tf_op jit(solution)/shard_map/all_gather | solution.py:137
  330.4 10.6 %multiply_reduce_fusion.1 = (f32[512]{0:T(512)S(1)}, f32[512]{0:T(512)S(1)}, f32[512,1024]{1,0:T(8,128)S(1)}) fusion(f32[512,1024]{1,0:T(8,128)} %reshape.531, bf16[512,1024]{1,0:T(8,128)(2,1)} %param.21, f32[1024]{0:T(1024)S(1)} %copy-done.15, bf16[512,4096]{1,0:T(8,128)(2,1)} %all-gather.8.cloned.1.call-done, ...), kind=kOutput, calls=%fused_computation.184 | convolution fusion | flops 4300733440 | bytes 17833984 | tf_op jit(solution)/shard_map/dot_general | solution.py:135
  341.0 3.6 fusion.104
  346.6 3.5 fusion.105
  350.1 13.9 %convolution_bitcast_fusion.4 = f32[4096,1024]{0,1:T(8,128)} fusion(bf16[512,4096]{1,0:T(8,128)(2,1)} %all-gather.8.cloned.1.call-done, f32[512]{0:T(512)S(1)} %get-tuple-element.1859, f32[1024]{0:T(1024)S(1)} %copy-done.15, f32[512,1024]{1,0:T(8,128)} %reshape.531, bf16[512,1024]{1,0:T(8,128)(2,1)} %param.21), kind=kOutput, calls=%fused_computation.168 | convolution fusion | flops 4299685888 | bytes 24123392 | tf_op jit(solution)/shard_map/td,ti->di/dot_general | solution.py:150
  368.8 3.1 copy.152
  371.8 132.6 %all-gather.14.cloned.1.call-done = f32[512,64,128]{2,1,0:T(8,128)} async-done(((f32[16,64,128]{2,1,0:T(8,128)}), f32[512,64,128]{2,1,0:T(8,128)}) %all-gather.14.cloned.1.call-update) | async-done | bytes 16777232 | tf_op jit(solution)/shard_map/all_gather | solution.py:15
  504.5 11.8 %rev.19 = f32[32,16,64,128]{3,2,1,0:T(8,128)} reverse(f32[32,16,64,128]{3,2,1,0:T(8,128)} %bitcast.594), dimensions={0} | reverse | bytes 33554432 | tf_op jit(solution)/shard_map/rev | solution.py:17
  516.3 37.7 %while.111 = (s32[]{:T(128)}, f32[16,64,128]{2,1,0:T(8,128)S(1)}, s32[]{:T(128)}, f32[32,16]{1,0:T(8,128)S(1)}, f32[32,16,64,128]{3,2,1,0:T(8,128)}) while((s32[]{:T(128)}, f32[16,64,128]{2,1,0:T(8,128)S(1)}, s32[]{:T(128)}, f32[32,16]{1,0:T(8,128)S(1)}, f32[32,16,64,128]{3,2,1,0:T(8,128)}) %tuple.234), condition=%wide.region_15.16_spmd.clone.clone, body=%wide.region_14.15_spmd.clone.sunk.clone | while | flops 524292 | bytes 1573145 | solution.py:27
  556.7 163.1 %while.108 = (s32[]{:T(128)}, f32[16,64,128]{2,1,0:T(8,128)S(1)}, bf16[4,128,16,64]{1,3,2,0:T(8,128)(2,1)}, bf16[4,128,1,128]{3,1,2,0:T(8,128)(2,1)}, bf16[4,128...) while((s32[]{:T(128)}, f32[16,64,128]{2,1,0:T(8,128)S(1)}, ...), condition=%wide.region_25.26_spmd.clone.clone, body=%wide.region_16.25_spmd.clone.sunk.clone | while | flops 1263466496 | bytes 32037560 | solution.py:67
  559.6 3.3 fusion.236
  567.2 5.0 fusion.238
  585.5 3.1 fusion.237
  600.3 3.3 fusion.236
  608.0 5.0 fusion.238
  626.3 3.1 fusion.237
  641.0 3.3 fusion.236
  648.7 5.0 fusion.238
  681.7 3.3 fusion.236
  689.3 5.0 fusion.238
  707.6 3.1 fusion.237
  (487 shorter events, 300.3 us)
Async XLA Ops:
  7.2 168.2 %all-gather.12.cloned.1.call-start = ((), (), s32[]{:S(2)}) async-start(), calls=%async_computation.4 | async-start | bytes 17301504 | tf_op jit(solution)/shard_map/all_gather | solution.py:15
  7.9 0.9 copy-start.16
  13.3 0.8 copy-start.5
  13.3 0.8 copy-start.13
  13.3 0.9 copy-start.3
  14.2 3.5 copy-start.12
  16.2 292.6 %all-gather.8.cloned.1.call-start = ((), (), s32[]{:S(2)}) async-start(), calls=%async_computation.1 | async-start | bytes 5242880 | tf_op jit(solution)/shard_map/all_gather | solution.py:133
  16.9 313.5 %all-gather.10.cloned.1.call-start = ((), (), s32[]{:S(2)}) async-start(), calls=%async_computation.2 | async-start | bytes 8650752 | tf_op jit(solution)/shard_map/all_gather | solution.py:137
  17.6 486.8 %all-gather.14.cloned.1.call-start = ((), (), s32[]{:S(2)}) async-start(), calls=%async_computation.5 | async-start | bytes 17301504 | tf_op jit(solution)/shard_map/all_gather | solution.py:15
  117.3 1.9 copy-start.4
  299.2 4.8 copy-start.1
  303.9 26.5 %copy-start.15 = (f32[1024]{0:T(1024)S(1)}, f32[1024]{0:T(1024)}, u32[]{:S(2)}) copy-start(f32[1024]{0:T(1024)} %param.28) | copy-start | bytes 12292
  330.4 10.6 %copy-start.2 = (f32[512,1024]{1,0:T(8,128)S(1)}, f32[512,1024]{1,0:T(8,128)}, u32[]{:S(2)}) copy-start(f32[512,1024]{1,0:T(8,128)} %reshape.531) | copy-start | bytes 6291460
  350.1 379.5 %reduce-scatter.2.cloned.1.call-start = ((), (), s32[]{:S(2)}) async-start(), calls=%async_computation.3 | async-start | bytes 17301504 | tf_op jit(solution)/shard_map/reduce_scatter | solution.py:149
  585.5 6.6 copy-start
  590.6 5.8 copy-start.9
  592.1 4.6 copy-start.7
  597.0 0.7 copy-start.8
  626.3 6.5 copy-start
  631.4 5.7 copy-start.9
  632.7 4.6 copy-start.7
  637.7 0.7 copy-start.8
  666.9 6.5 copy-start
  672.0 5.8 copy-start.9
  673.4 4.6 copy-start.7
  707.6 6.6 copy-start
  712.8 5.8 copy-start.9
  714.2 4.6 copy-start.7
  723.5 2.3 copy-start.6
  723.5 2.3 copy-start.11
  723.5 2.3 copy-start.14
  723.5 2.3 copy-start.17
  (6 other events, 4.0 us)
Sparse Core Ops, SparseCore 0:
  16.3 159.0 all-gather.11
  177.0 43.7 all-gather.7
  223.9 106.4 all-gather.9
  350.2 154.2 all-gather.13
  506.7 222.8 reduce-scatter.1
where the time goes:
time: 749 us; the launch traced here: 738 us
  waiting for transfers between devices  213 us (28%)
  other arithmetic  151 us (20%)
  local copies, waits for them, and re-layouts  131 us (17%)
  matrix products  131 us (17%)
  blocking collectives  96 us (13%)
  between operations  14.4 us (2%)
    all_gather x2, waiting for transfers between devices, prefix(): pieces = jax.tree.map(lambda part: lax.all_gather(part, axis), value)  187 us
    all_gather x1, blocking collectives, prefix(): pieces = jax.tree.map(lambda part: lax.all_gather(part, axis), value)  96 us
    select_n x62, other arithmetic, step(): jnp.where(position < mine, new, old)  73.1 us
    dot_general x12, matrix products, block_step(): within = jnp.einsum('hts,shp->thp', mixing, x_block, precision=highest)  47 us
    dynamic_update_slice x24, other arithmetic, scan_blocks(): lax.scan(stepper, start, (x_blocks, b_blocks, c_blocks, rate_blocks, step...  26.9 us
    dynamic_slice x20, local copies, waits for them, and re-layouts, scan_blocks(): lax.scan(stepper, start, (x_blocks, b_blocks, c_blocks, rate_blocks, step...  25.7 us
    dot_general x12, matrix products, block_step(): jnp.einsum('thn,hpn->thp', c_heads, carried, precision=highest)  25.6 us
    dot_general x12, matrix products, block_step(): jnp.einsum('sh,shp,shn->hpn', weighted, x_block, b_heads, precision=highest)  25.3 us
  transfers between devices with their start and end apart: 5, of which 4 were waited for; matrix products, arithmetic and copies ran while one was open for 51% of the time, Pallas kernels for 0%

commit v1 on v0

--- a/solution.py
+++ b/solution.py
@@ -134,7 +134,9 @@
     columns = gathered
     d_normed = jnp.dot(
         columns,
-        lax.all_gather(out_weight, "seq", axis=0, tiled=True),
+        jnp.concatenate(
+            lax.all_to_all(jnp.stack([out_weight] * lax.axis_size("seq")), "seq", 0, 0), axis=0
+        ),
         preferred_element_type=jnp.float32,
     )
     d_mixed, grad_z = norm_pull(d_normed)

time: 749 us -> 821 us (1.096)
  blocking collectives: 96 us -> 211 us
  waiting for transfers between devices: 213 us -> 155 us
  starting transfers between devices: 0.2 us -> 11.1 us
    all_gather x1, blocking collectives: 96 us -> 211 us  [prefix(): pieces = jax.tree.map(lambda part: lax.all_gather(part, axis), value)]
    all_gather x2, waiting for transfers between devices: 187 us -> 152 us  [prefix(): pieces = jax.tree.map(lambda part: lax.all_gather(part, axis), value)]
    all_gather x1 -> x0, waiting for transfers between devices: 21.7 us -> none  [body(): lax.all_gather(out_weight, 'seq', axis=0, tiled=True)]
    all_to_all x0 -> x1, starting transfers between devices: none -> 11 us  [body(): lax.all_to_all(jnp.stack([out_weight] * lax.axis_size('seq')), 'seq', 0, 0)]
  transfers between devices with their start and end apart: 5 -> 5, of which waited for: 4 -> 3; matrix products, arithmetic and copies ran while one was open for 51% -> 47% of each run, Pallas kernels for 0% -> 0%
where the time goes in v1:
time: 821 us; the launch traced here: 810 us
  blocking collectives  211 us (26%)
  waiting for transfers between devices  155 us (19%)
  other arithmetic  149 us (18%)
  local copies, waits for them, and re-layouts  135 us (16%)
  matrix products  131 us (16%)
  between operations  14.4 us (2%)
  starting transfers between devices  11.1 us (1%)
    all_gather x1, blocking collectives, prefix(): pieces = jax.tree.map(lambda part: lax.all_gather(part, axis), value)  211 us
    all_gather x2, waiting for transfers between devices, prefix(): pieces = jax.tree.map(lambda part: lax.all_gather(part, axis), value)  152 us
    select_n x62, other arithmetic, step(): jnp.where(position < mine, new, old)  73.1 us
    dot_general x12, matrix products, block_step(): within = jnp.einsum('hts,shp->thp', mixing, x_block, precision=highest)  46.9 us
    dynamic_update_slice x24, other arithmetic, scan_blocks(): lax.scan(stepper, start, (x_blocks, b_blocks, c_blocks, rate_blocks, step...  26.5 us
    dynamic_slice x20, local copies, waits for them, and re-layouts, scan_blocks(): lax.scan(stepper, start, (x_blocks, b_blocks, c_blocks, rate_blocks, step...  25.7 us
    dot_general x12, matrix products, block_step(): jnp.einsum('thn,hpn->thp', c_heads, carried, precision=highest)  25.6 us
    dot_general x12, matrix products, block_step(): jnp.einsum('sh,shp,shn->hpn', weighted, x_block, b_heads, precision=highest)  25.3 us
  transfers between devices with their start and end apart: 5, of which 3 were waited for; matrix products, arithmetic and copies ran while one was open for 47% of the time, Pallas kernels for 0%

profile of v1, /device:TPU:0, one launch (start us, length us, event | category | flops | bytes accessed | tf_op | source)
XLA Modules:
  0.0 809.7 jit_solution(17563684810643973997)
XLA Ops:
  16.2 4.3 stack.2
  20.4 11.0 %all-to-all-start = ((bf16[32,128,1024]{2,1,0:T(8,128)(2,1)}), bf16[32,128,1024]{2,1,0:T(8,128)(2,1)}, u32[]{:S(2)}, u32[]{:S(2)}) async-start(bf16[32,128,1024]{2,1,0:T(8,128)(2,1)} %stack.2), calls=%async_computation | async-start | bytes 16777216 | tf_op jit(solution)/shard_map/all_to_all | solution.py:138
  35.8 211.2 %all-gather.2 = f32[32,1,16]{2,1,0:T(1,128)S(1)} all-gather(f32[1,1,16]{2,1,0:T(1,128)S(1)} %fusion.127), channel_id=1, replica_groups=mesh['seq'=32,'head'=4] {'seq'}, dimensions={0}, use_global_device_ids=true | all-gather | bytes 2112 | tf_op jit(solution)/shard_map/all_gather | solution.py:15
  250.7 19.5 %all-gather.9.cloned.1.call-done = f32[512,64,128]{2,1,0:T(8,128)} async-done(((f32[16,64,128]{2,1,0:T(8,128)}), f32[512,64,128]{2,1,0:T(8,128)}) %all-gather.9.cloned.1.call-update) | async-done | bytes 16777232 | tf_op jit(solution)/shard_map/all_gather | solution.py:15
  270.1 37.9 %while.110 = (s32[]{:T(128)}, f32[16,64,128]{2,1,0:T(8,128)S(1)}, s32[]{:T(128)}, f32[32,16]{1,0:T(8,128)S(1)}, f32[32,16,64,128]{3,2,1,0:T(8,128)}) while((s32[]{:T(128)}, f32[16,64,128]{2,1,0:T(8,128)S(1)}, s32[]{:T(128)}, f32[32,16]{1,0:T(8,128)S(1)}, f32[32,16,64,128]{3,2,1,0:T(8,128)}) %tuple.252), condition=%wide.region_8.9_spmd.clone.clone, body=%wide.region_7.8_spmd.clone.sunk.clone | while | flops 524292 | bytes 1573145 | solution.py:27
  310.8 82.7 %while.109 = (s32[]{:T(128)}, f32[16,64,128]{2,1,0:T(8,128)S(1)}, f32[4,128,16,64]{1,3,2,0:T(8,128)}, f32[4,16,128,128]{3,2,1,0:T(8,128)}, f32[4,16,128,128]{3,2...) while((s32[]{:T(128)}, f32[16,64,128]{2,1,0:T(8,128)S(1)}, ...), condition=%wide.region_11.12_spmd.clone.clone.clone, body=%wide.region_9.11_spmd.clone.clone.sunk.clone | while | flops 633511936 | bytes 16000793 | solution.py:67
  319.9 3.7 fusion.254
  340.6 3.7 fusion.254
  361.3 3.7 fusion.254
  381.8 3.7 fusion.254
  393.5 4.8 copy.179
  398.3 4.9 reshape.537
  403.2 10.6 %multiply_reduce_fusion.1 = (f32[512]{0:T(512)S(1)}, f32[512]{0:T(512)S(1)}, f32[512,1024]{1,0:T(8,128)S(1)}) fusion(f32[512,1024]{1,0:T(8,128)} %reshape.537, bf16[512,1024]{1,0:T(8,128)(2,1)} %param.21, f32[1024]{0:T(1024)S(1)} %copy-done.17, bf16[512,4096]{1,0:T(8,128)(2,1)} %all-gather.7.cloned.1.call-done, bf16[4096,1024]{1,0:T(8,128)(2,1)} %bitcast.6), kind=kOutput, calls=%fused_computation.184 | convolution fusion | flops 4300733440 | bytes 17833984 | tf_op jit(solution)/shard_map/dot_general | solution.py:135
  418.4 3.5 fusion.105
  422.0 13.9 %convolution_bitcast_fusion.4 = f32[4096,1024]{0,1:T(8,128)} fusion(bf16[512,4096]{1,0:T(8,128)(2,1)} %all-gather.7.cloned.1.call-done, f32[512]{0:T(512)S(1)} %get-tuple-element.1859, f32[1024]{0:T(1024)S(1)} %copy-done.17, f32[512,1024]{1,0:T(8,128)} %reshape.537, bf16[512,1024]{1,0:T(8,128)(2,1)} %param.21), kind=kOutput, calls=%fused_computation.168 | convolution fusion | flops 4299685888 | bytes 24123392 | tf_op jit(solution)/shard_map/td,ti->di/dot_general | solution.py:152
  440.6 3.1 copy.152
  443.7 132.6 %all-gather.11.cloned.1.call-done = f32[512,64,128]{2,1,0:T(8,128)} async-done(((f32[16,64,128]{2,1,0:T(8,128)}), f32[512,64,128]{2,1,0:T(8,128)}) %all-gather.11.cloned.1.call-update) | async-done | bytes 16777232 | tf_op jit(solution)/shard_map/all_gather | solution.py:15
  576.3 11.8 %rev.19 = f32[32,16,64,128]{3,2,1,0:T(8,128)} reverse(f32[32,16,64,128]{3,2,1,0:T(8,128)} %bitcast.595), dimensions={0} | reverse | bytes 33554432 | tf_op jit(solution)/shard_map/rev | solution.py:17
  588.1 37.7 %while.111 = (s32[]{:T(128)}, f32[16,64,128]{2,1,0:T(8,128)S(1)}, s32[]{:T(128)}, f32[32,16]{1,0:T(8,128)S(1)}, f32[32,16,64,128]{3,2,1,0:T(8,128)}) while((s32[]{:T(128)}, f32[16,64,128]{2,1,0:T(8,128)S(1)}, s32[]{:T(128)}, f32[32,16]{1,0:T(8,128)S(1)}, f32[32,16,64,128]{3,2,1,0:T(8,128)}) %tuple.234), condition=%wide.region_15.16_spmd.clone.clone, body=%wide.region_14.15_spmd.clone.sunk.clone | while | flops 524292 | bytes 1573145 | solution.py:27
  628.5 163.1 %while.108 = (s32[]{:T(128)}, f32[16,64,128]{2,1,0:T(8,128)S(1)}, bf16[4,128,16,64]{1,3,2,0:T(8,128)(2,1)}, bf16[4,128,1,128]{3,1,2,0:T(8,128)(2,1)}, bf16[4,128...) while((s32[]{:T(128)}, f32[16,64,128]{2,1,0:T(8,128)S(1)}, ...), condition=%wide.region_25.26_spmd.clone.clone, body=%wide.region_16.25_spmd.clone.sunk.clone | while | flops 1263466496 | bytes 32037560 | solution.py:67
  631.4 3.3 fusion.236
  639.1 5.0 fusion.238
  657.4 3.1 fusion.237
  672.2 3.3 fusion.236
  679.8 4.9 fusion.238
  698.1 3.1 fusion.237
  712.9 3.3 fusion.236
  720.5 5.0 fusion.238
  738.8 3.1 fusion.237
  753.6 3.3 fusion.236
  761.2 5.0 fusion.238
  779.5 3.1 fusion.237
  (491 shorter events, 301.5 us)
Async XLA Ops:
  7.2 263.0 %all-gather.9.cloned.1.call-start = ((), (), s32[]{:S(2)}) async-start(), calls=%async_computation.4 | async-start | bytes 17301504 | tf_op jit(solution)/shard_map/all_gather | solution.py:15
  7.9 0.9 copy-start.18
  13.3 0.8 copy-start.6
  13.3 0.8 copy-start.15
  13.3 0.9 copy-start.4
  13.6 2.6 copy-start.8
  20.4 11.8 %copy-start.14 = (s32[16,4]{0,1:T(4,128)S(1)}, s32[16,4]{0,1:T(4,128)}, u32[]{:S(2)}) copy-start(s32[16,4]{0,1:T(4,128)} %param.29) | copy-start | bytes 772
  20.4 382.7 %all-to-all-start = ((bf16[32,128,1024]{2,1,0:T(8,128)(2,1)}), bf16[32,128,1024]{2,1,0:T(8,128)(2,1)}, u32[]{:S(2)}, u32[]{:S(2)}) async-start(bf16[32,128,1024]{2,1,0:T(8,128)(2,1)} %stack.2), calls=%async_computation | async-start | bytes 16777216 | tf_op jit(solution)/shard_map/all_to_all | solution.py:138
  31.4 371.7 %all-gather.7.cloned.1.call-start = ((), (), s32[]{:S(2)}) async-start(), calls=%async_computation.2 | async-start | bytes 5242880 | tf_op jit(solution)/shard_map/all_gather | solution.py:133
  32.2 544.1 %all-gather.11.cloned.1.call-start = ((), (), s32[]{:S(2)}) async-start(), calls=%async_computation.5 | async-start | bytes 17301504 | tf_op jit(solution)/shard_map/all_gather | solution.py:15
  247.0 1.9 copy-start.5
  393.5 4.8 copy-start.1
  398.3 4.9 copy-start.17
  403.2 10.6 %copy-start.2 = (f32[512,1024]{1,0:T(8,128)S(1)}, f32[512,1024]{1,0:T(8,128)}, u32[]{:S(2)}) copy-start(f32[512,1024]{1,0:T(8,128)} %reshape.537) | copy-start | bytes 6291460
  403.2 10.6 %copy-start.3 = (bf16[512,1024]{1,0:T(8,128)(2,1)S(1)}, bf16[512,1024]{1,0:T(8,128)(2,1)}, u32[]{:S(2)}) copy-start(bf16[512,1024]{1,0:T(8,128)(2,1)} %param.21) | copy-start | bytes 3145732
  421.9 379.0 %reduce-scatter.2.cloned.1.call-start = ((), (), s32[]{:S(2)}) async-start(), calls=%async_computation.3 | async-start | bytes 17301504 | tf_op jit(solution)/shard_map/reduce_scatter | solution.py:151
  657.4 6.6 copy-start
  662.5 5.8 copy-start.11
  663.9 4.6 copy-start.9
  698.1 6.5 copy-start
  703.2 5.7 copy-start.11
  704.6 4.6 copy-start.9
  738.8 6.5 copy-start
  743.9 5.7 copy-start.11
  745.3 4.6 copy-start.9
  779.5 6.5 copy-start
  784.7 5.8 copy-start.11
  786.1 4.6 copy-start.9
  795.4 2.3 copy-start.7
  795.4 2.3 copy-start.13
  795.4 2.3 copy-start.16
  795.4 2.3 copy-start.19
  (8 other events, 5.3 us)
Sparse Core Ops, SparseCore 0:
  16.3 253.8 all-gather.8
  271.8 43.7 all-gather.6
  422.0 154.2 all-gather.10
  578.6 222.3 reduce-scatter.1
